TPU v7x, 256 devices: a whole 4x4x8 slice. The times are simulated.
256 devices in a mesh: comp: 2 (over core), lat: 32 (over y, z), lon: 4 (over x).
Axes of the slice: x: 4, y: 4, z: 8, core: 2. Of those that a mesh axis runs over, the one named last changes fastest.
Arguments:
- increment: float32 [2, 8, 512, 2048], P('comp', None, 'lat', 'lon'), may hold values from -6 to 6
- diffusivity: float32 [2, 8, 512, 2048], P('comp', None, 'lat', 'lon'), may hold values from 0.03 to 0.24
- innovation: float32 [2, 8, 512, 2048], P('comp', None, 'lat', 'lon'), may hold values from -6 to 6
- land_mask: int32 [512, 2048], P('lat', 'lon'), may hold values 0 or 1
- pull_cells: int32 [2, 32, 4, 32, 1024], P('comp', 'lat', 'lon'), may hold values from 0 to 8191
- put_cells: int32 [2, 32, 4, 32, 1024], P('comp', 'lat', 'lon'), may hold values from 0 to 8191
- pull_weight: float32 [2, 32, 4, 32, 1024], P('comp', 'lat', 'lon'), may hold values from 0.2 to 0.8
- pull_count: int32 [2, 32, 4, 32], P('comp', 'lat', 'lon'), may hold values from 1 to 1024, 16384 in all within a row
Outputs:
- linear_state: float32 [2, 8, 512, 2048], P('comp', None, 'lat', 'lon')
- gradient: float32 [2, 8, 512, 2048], P('comp', None, 'lat', 'lon')
Inputs may be any that keep to these rules, and one draw needn't show every extreme that they name: `pull_count`: for each receiving block the counts over the 32 source bands add up to 16384, and the largest of them is 1024.
All inputs are finite; a program needn't handle non-finite values. No bound on the sum of `land_mask` on one device may be relied on, other than what follows from the above.
Results may differ from a plain program's by a relative error of at most 0.00002.
Values sent between devices are 32-bit elements; how exact they have to be, the bound alone decides.
No kernel may reach another device: no remote copies, remote signals or barrier semaphores. Data moves between devices by JAX's collectives and lax.ppermute only.
A program may use at most 64 MiB of HBM per device.

v0:
```python
import jax
import jax.numpy as jnp
from jax import lax
from jax.sharding import PartitionSpec as P

NSTEP = 4


def partner_2(value, axis, stride):
    mask = 2**stride
    pairs = [(source, source ^ mask) for source in range(lax.axis_size(axis))]
    return lax.ppermute(value, axis, pairs)


def extended(cells, sides, width, closed):
    for axis, dim in sides:
        count = lax.axis_size(axis)
        ends = count if closed else count - 1
        head = lax.slice_in_dim(cells, 0, width, axis=dim)
        tail = lax.slice_in_dim(cells, cells.shape[dim] - width, cells.shape[dim], axis=dim)
        cells = jnp.concatenate(
            [
                lax.ppermute(tail, axis, [(i, (i + 1) % count) for i in range(ends)]),
                cells,
                lax.ppermute(head, axis, [((i + 1) % count, i) for i in range(ends)]),
            ],
            axis=dim,
        )
    return cells


def mirrored(rows):
    partner = rows
    for bit in range(lax.axis_size("lon").bit_length() - 1):
        partner = partner_2(partner, "lon", bit)
    return partner[:, :, :, ::-1]


def at_fold():
    return (lax.axis_index("comp") == 1) & (lax.axis_index("lat") == lax.axis_size("lat") - 1)


def neighbours(field):
    lat_padded = extended(field, (("lat", 2),), 1, False)
    lon_padded = extended(field, (("lon", 3),), 1, True)
    folded = mirrored(field[:, :, -1:, :])[:, :, 0, :]
    north_edge = jnp.where(at_fold(), folded, lat_padded[:, :, -1, :])
    north = jnp.concatenate([lat_padded[:, :, 2:-1, :], north_edge[:, :, None, :]], axis=2)
    east = lon_padded[:, :, :, 2:]
    west = lon_padded[:, :, :, :-2]
    south = lat_padded[:, :, :-2, :]
    return (east, west, south, north)


def advance(field, coefficients):
    east, west, south, north = neighbours(field)
    change = coefficients[0] * (east - field) + coefficients[1] * (west - field)
    change = change + coefficients[2] * (south - field)
    change = change + coefficients[3] * (north - field)
    return field + change


def local(
    increment, diffusivity, innovation, land_mask, pull_cells, put_cells, pull_weight, pull_count
):
    height = increment.shape[2]
    width = increment.shape[3]
    cells = height * width
    bands = lax.axis_size("lat")
    ocean = lax.axis_index("comp") == 1
    mask_plane = jnp.where(
        ocean, land_mask.astype(jnp.float32), jnp.ones_like(land_mask, jnp.float32)
    )
    mask_levels = mask_plane[None, None]
    stacked = jnp.concatenate([diffusivity, mask_levels], axis=1)
    near = neighbours(stacked)
    coefficients = [
        mask_levels * side[:, -1:] * 0.5 * (diffusivity + side[:, :-1]) for side in near
    ]

    def sweep(field):
        for step in range(NSTEP):
            field = advance(field, coefficients)
        return field

    pulled = pull_cells.reshape(bands, -1)
    placed = put_cells.reshape(bands, -1)
    slot_count = pulled.shape[1]
    live = jnp.arange(slot_count, dtype=jnp.int32)[None, :] < pull_count.reshape(bands, 1)
    live_weight = jnp.where(
        live, pull_weight.reshape(bands, -1), jnp.zeros((bands, slot_count), jnp.float32)
    )
    mask_flat = mask_plane.reshape(-1)
    state = sweep(increment)
    surface = mask_flat * state[0, 0].reshape(-1)
    other_surface = partner_2(surface[None, :], "comp", 0)
    chosen = pulled
    values = jnp.take_along_axis(
        lax.all_gather(other_surface, "lat", axis=0, tiled=True), chosen, axis=1
    )
    income = jax.ops.segment_sum(
        (live_weight * values).reshape(-1), placed.reshape(-1), num_segments=cells
    )
    linear_state = state.at[0, 0].add((mask_flat * income).reshape(height, width))
    residual = linear_state - innovation
    residual_surface = mask_flat * residual[0, 0].reshape(-1)
    outgoing = live_weight * jnp.take(residual_surface, placed)
    chosen = pulled
    segment_ids = chosen + (jnp.arange(1 * lax.axis_size("lat"), dtype=jnp.int32) * cells)[:, None]
    summed = jax.ops.segment_sum(
        outgoing.reshape(-1), segment_ids.reshape(-1), num_segments=1 * lax.axis_size("lat") * cells
    )
    band_sums = lax.psum_scatter(
        summed.reshape(1 * lax.axis_size("lat"), cells), "lat", scatter_dimension=0, tiled=True
    )
    returned = partner_2(band_sums, "comp", 0)[0]
    adjoint_state = residual.at[0, 0].add((mask_flat * returned).reshape(height, width))
    adjoint_state = sweep(adjoint_state)
    gradient = adjoint_state + increment
    return (linear_state, gradient)


def solution(mesh):
    placed = (
        P("comp", None, "lat", "lon"),
        P("comp", None, "lat", "lon"),
        P("comp", None, "lat", "lon"),
        P("lat", "lon"),
        P("comp", "lat", "lon", None, None),
        P("comp", "lat", "lon", None, None),
        P("comp", "lat", "lon", None, None),
        P("comp", "lat", "lon", None),
    )
    return jax.shard_map(
        local,
        mesh=mesh,
        in_specs=placed,
        out_specs=(P("comp", None, "lat", "lon"), P("comp", None, "lat", "lon")),
        check_vma=False,
    )
```

profile of v0, /device:TPU:8, one launch (start us, length us, event | category | flops | bytes accessed | tf_op | source)
XLA Modules:
  0.0 1201.9 jit_solution(17627987960869966401)
XLA Ops:
  9.0 1.6 collective-permute-start.6
  10.6 3.8 collective-permute-start.4
  16.1 3.8 collective-permute-start.5
  19.9 4.1 collective-permute-start.11
  26.0 3.1 collective-permute-start.10
  29.2 2.1 collective-permute-done.10
  31.3 3.6 collective-permute-start.8
  35.4 2.8 collective-permute-start
  39.0 4.6 collective-permute-done.7
  44.1 3.3 collective-permute-start.1
  47.5 1.7 collective-permute-done.2
  49.3 3.7 collective-permute-done.3
  53.5 3.9 collective-permute-start.17
  57.5 1.4 collective-permute-start.16
  59.0 1.9 collective-permute-start.14
  60.9 3.4 collective-permute-start.12
  64.8 1.4 collective-permute-done.12
  66.3 3.6 collective-permute-done.13
  70.2 6.0 collective-permute-start.23
  76.3 1.5 collective-permute-start.22
  77.9 1.9 collective-permute-start.20
  79.8 3.3 collective-permute-start.18
  83.6 1.4 collective-permute-done.18
  85.1 3.6 collective-permute-done.19
  89.1 6.0 collective-permute-start.29
  95.1 1.5 collective-permute-start.28
  96.8 1.9 collective-permute-start.26
  98.7 3.3 collective-permute-start.24
  102.5 1.4 collective-permute-done.24
  103.9 3.6 collective-permute-done.25
  108.0 1.2 collective-permute-done.30
  111.5 71.1 %all-gather.3.cloned.1.call-done = f32[32,1,8192]{2,1,0:T(1,128)} async-done(((f32[1,1,8192]{2,1,0:T(1,128)}), f32[32,1,8192]{2,1,0:T(1,128)}) %all-gather.3.cloned.1.call-update) | async-done | bytes 1048592 | tf_op jit(solution)/shard_map/all_gather | solution.py:99
  182.6 1.8 copy.24
  184.4 258.4 %gather_fusion.1 = f32[32768]{0:T(1024)S(1)} fusion(f32[32,8192]{1,0:T(8,128)S(1)} %bitcast.88, s32[32768]{0:T(1024)S(1)} %bitcast.89), kind=kCustom, calls=%fused_computation.1 | custom fusion | bytes 524288 | tf_op jit(solution)/shard_map/jit(take_along_axis)/gather | solution.py:98
  442.9 171.1 %scatter_custom_fusion = f32[8192]{0:T(1024)S(1)} fusion(s32[32768]{0:T(1024)S(1)} %bitcast.94, f32[32768]{0:T(1024)S(1)} %select_multiply_fusion.1, f32[]{:T(128)} %constant.98.clone.1), kind=kCustom, calls=%fused_computation.200 | custom fusion | flops 32768 | bytes 32772 | tf_op jit(solution)/shard_map/scatter-add | solution.py:101
  615.2 180.5 %gather_fusion = f32[32768]{0:T(1024)S(1)} fusion(f32[8192]{0:T(1024)S(1)} %mul.242, s32[32768]{0:T(1024)S(1)} %broadcast_clamp_fusion), kind=kCustom, calls=%fused_computation | custom fusion | bytes 393216 | tf_op jit(solution)/shard_map/jit(_take)/gather | solution.py:107
  795.8 171.6 %scatter_custom_fusion.1 = f32[262144]{0:T(1024)S(1)} fusion(s32[32768]{0:T(1024)} %bitcast.105, f32[32768]{0:T(1024)S(1)} %select_multiply_fusion, f32[]{:T(128)} %constant.98.clone.1), kind=kCustom, calls=%fused_computation.9 | custom fusion | flops 32768 | bytes 1049088 | tf_op jit(solution)/shard_map/scatter-add | solution.py:110
  969.8 145.8 %all-reduce.3.cloned.1.call-done = f32[32,8192]{1,0:T(8,128)} async-done(((f32[32,8192]{1,0:T(8,128)}), f32[32,8192]{1,0:T(8,128)}) %all-reduce.3.cloned.1.call-update) | async-done | bytes 1048592
  1115.6 1.6 constant_dynamic-slice_fusion
  1119.8 1.6 collective-permute-start.35
  1121.4 4.9 collective-permute-start.37
  1126.4 2.8 collective-permute-start.36
  1129.2 1.9 collective-permute-start.34
  1132.0 1.5 collective-permute-start.33
  1134.0 1.8 collective-permute-done.32
  1135.7 1.8 collective-permute-done.33
  1138.1 6.0 collective-permute-start.43
  1144.2 1.3 collective-permute-start.42
  1145.6 1.9 collective-permute-start.40
  1147.5 3.3 collective-permute-start.38
  1151.3 1.4 collective-permute-done.38
  1152.7 3.6 collective-permute-done.39
  1156.7 6.0 collective-permute-start.49
  1162.7 1.5 collective-permute-start.48
  1164.4 1.9 collective-permute-start.46
  1166.3 3.3 collective-permute-start.44
  1170.1 1.4 collective-permute-done.44
  1171.5 3.6 collective-permute-done.45
  1175.5 6.2 collective-permute-start.55
  1181.7 1.4 collective-permute-start.54
  1183.2 1.9 collective-permute-start.52
  1185.1 3.5 collective-permute-start.50
  1189.1 1.4 collective-permute-done.50
  1190.5 3.6 collective-permute-done.51
  (170 shorter events, 24.7 us)
Async XLA Ops:
  7.2 21.9 %copy-start = (f32[1,8,16,512]{3,2,1,0:T(8,128)S(1)}, f32[1,8,16,512]{3,2,1,0:T(8,128)}, u32[]{:S(2)}) copy-start(f32[1,8,16,512]{3,2,1,0:T(8,128)} %param.13) | copy-start | bytes 786436
  7.2 22.0 %copy-start.1 = (f32[1,8,16,512]{3,2,1,0:T(8,128)S(1)}, f32[1,8,16,512]{3,2,1,0:T(8,128)}, u32[]{:S(2)}) copy-start(f32[1,8,16,512]{3,2,1,0:T(8,128)} %param.12) | copy-start | bytes 786436
  7.2 175.4 %all-gather.3.cloned.1.call-start = ((), (), s32[]{:S(2)}) async-start(), calls=%async_computation | async-start | bytes 1081344 | tf_op jit(solution)/shard_map/all_gather | solution.py:99
  9.0 29.2 %collective-permute-start.6 = (f32[1,9,1,512]{3,2,1,0:T(1,128)S(1)}, f32[1,9,1,512]{3,2,1,0:T(1,128)S(1)}, u32[]{:S(2)}, u32[]{:S(2)}) collective-permute-start(f32[1,9,1,512]{3,2,1,0:T(1,128)S(1)} %get-tuple-element.37), channel_id=1, source_target_pairs={{0,1},{1,0},{2,3},{3,2},{4,5},{5,4},{6,7},{7,6},{8,9},{9,8},{10,11... | collective-permute-start | bytes 55304 | tf_op jit(solution)/shard_map/ppermute | solution.py:12
  10.6 38.5 %collective-permute-start.4 = (f32[1,9,1,512]{3,2,1,0:T(1,128)S(1)}, f32[1,9,1,512]{3,2,1,0:T(1,128)S(1)}, u32[]{:S(2)}, u32[]{:S(2)}) collective-permute-start(f32[1,9,1,512]{3,2,1,0:T(1,128)S(1)} %get-tuple-element.37), channel_id=1, source_target_pairs={{0,4},{4,8},{8,12},{12,16},{16,20},{20,24},{24,28},{28,32},{32,36}... | collective-permute-start | bytes 55304 | tf_op jit(solution)/shard_map/ppermute | solution.py:23
  15.4 10.5 collective-permute-start.9
  16.1 36.9 %collective-permute-start.5 = (f32[1,8,1,512]{3,2,1,0:T(1,128)S(1)}, f32[1,8,1,512]{3,2,1,0:T(1,128)S(1)}, u32[]{:S(2)}, u32[]{:S(2)}) collective-permute-start(f32[1,8,1,512]{3,2,1,0:T(1,128)S(1)} %get-tuple-element.67), channel_id=1, source_target_pairs={{0,4},{4,8},{8,12},{12,16},{16,20},{20,24},{24,28},{28,32},{32,36}... | collective-permute-start | bytes 49160 | tf_op jit(solution)/shard_map/ppermute | solution.py:23
  19.9 15.5 %collective-permute-start.11 = (f32[1,8,1,512]{3,2,1,0:T(1,128)S(1)}, f32[1,8,1,512]{3,2,1,0:T(1,128)S(1)}, u32[]{:S(2)}, u32[]{:S(2)}) collective-permute-start(f32[1,8,1,512]{3,2,1,0:T(1,128)S(1)} %get-tuple-element.66), channel_id=1, source_target_pairs={{4,0},{8,4},{12,8},{16,12},{20,16},{24,20},{28,24},{32,28},{36,32}... | collective-permute-start | bytes 49160 | tf_op jit(solution)/shard_map/ppermute | solution.py:25
  26.0 5.3 collective-permute-start.10
  31.3 12.8 %collective-permute-start.8 = (f32[1,9,1,512]{3,2,1,0:T(1,128)S(1)}, f32[1,9,1,512]{3,2,1,0:T(1,128)S(1)}, u32[]{:S(2)}, u32[]{:S(2)}) collective-permute-start(f32[1,9,1,512]{3,2,1,0:T(1,128)S(1)} %get-tuple-element.36), channel_id=1, source_target_pairs={{4,0},{8,4},{12,8},{16,12},{20,16},{24,20},{28,24},{32,28},{36,32}... | collective-permute-start | bytes 55304 | tf_op jit(solution)/shard_map/ppermute | solution.py:25
  35.4 12.0 collective-permute-start
  38.2 5.4 collective-permute-start.7
  43.6 5.6 collective-permute-start.2
  44.1 5.2 collective-permute-start.1
  47.4 5.6 collective-permute-start.3
  53.4 4.0 collective-permute-start.15
  53.5 11.3 collective-permute-start.17
  57.5 6.9 collective-permute-start.16
  59.0 10.8 collective-permute-start.14
  60.9 5.3 collective-permute-start.12
  64.4 5.5 collective-permute-start.13
  70.1 6.1 collective-permute-start.21
  70.2 13.4 %collective-permute-start.23 = (f32[1,8,1,512]{3,2,1,0:T(1,128)S(1)}, f32[1,8,1,512]{3,2,1,0:T(1,128)S(1)}, u32[]{:S(2)}, u32[]{:S(2)}) collective-permute-start(f32[1,8,1,512]{3,2,1,0:T(1,128)S(1)} %get-tuple-element.58), channel_id=1, source_target_pairs={{4,0},{8,4},{12,8},{16,12},{20,16},{24,20},{28,24},{32,28},{36,32}... | collective-permute-start | bytes 49160 | tf_op jit(solution)/shard_map/ppermute | solution.py:25
  76.3 6.9 collective-permute-start.22
  77.9 10.7 collective-permute-start.20
  79.8 5.2 collective-permute-start.18
  83.2 5.5 collective-permute-start.19
  88.9 6.2 collective-permute-start.27
  89.1 13.4 %collective-permute-start.29 = (f32[1,8,1,512]{3,2,1,0:T(1,128)S(1)}, f32[1,8,1,512]{3,2,1,0:T(1,128)S(1)}, u32[]{:S(2)}, u32[]{:S(2)}) collective-permute-start(f32[1,8,1,512]{3,2,1,0:T(1,128)S(1)} %get-tuple-element.54), channel_id=1, source_target_pairs={{4,0},{8,4},{12,8},{16,12},{20,16},{24,20},{28,24},{32,28},{36,32}... | collective-permute-start | bytes 49160 | tf_op jit(solution)/shard_map/ppermute | solution.py:25
  95.1 6.9 collective-permute-start.28
  96.8 10.7 collective-permute-start.26
  98.7 5.2 collective-permute-start.24
  102.0 5.5 collective-permute-start.25
  107.5 2.5 copy-start.5
  107.5 2.5 copy-start.8
  107.9 1.3 collective-permute-start.30
  109.8 1005.8 %all-reduce.3.cloned.1.call-start = ((), (), s32[]{:S(2)}) async-start(), calls=%async_computation.1 | async-start | bytes 2097152
  614.0 181.7 %copy-start.2 = (f32[1,8,16,512]{3,2,1,0:T(8,128)}, f32[1,8,16,512]{3,2,1,0:T(8,128)S(1)}, u32[]{:S(2)}) copy-start(f32[1,8,16,512]{3,2,1,0:T(8,128)S(1)} %add_dynamic-update-slice_fusion) | copy-start | bytes 786436
  968.5 151.2 %copy-start.6 = (s32[16,512]{1,0:T(8,128)S(1)}, s32[16,512]{1,0:T(8,128)}, u32[]{:S(2)}) copy-start(s32[16,512]{1,0:T(8,128)} %param.15) | copy-start | bytes 98308
  1117.2 1.3 collective-permute-start.31
  1119.8 6.5 collective-permute-start.35
  1121.4 12.5 %collective-permute-start.37 = (f32[1,8,1,512]{3,2,1,0:T(1,128)S(1)}, f32[1,8,1,512]{3,2,1,0:T(1,128)S(1)}, u32[]{:S(2)}, u32[]{:S(2)}) collective-permute-start(f32[1,8,1,512]{3,2,1,0:T(1,128)S(1)} %get-tuple-element.50), channel_id=1, source_target_pairs={{4,0},{8,4},{12,8},{16,12},{20,16},{24,20},{28,24},{32,28},{36,32}... | collective-permute-start | bytes 49160 | tf_op jit(solution)/shard_map/ppermute | solution.py:25
  1126.4 7.1 collective-permute-start.36
  1129.2 8.3 collective-permute-start.34
  1131.2 4.6 collective-permute-start.32
  1132.0 5.5 collective-permute-start.33
  1137.8 6.4 collective-permute-start.41
  1138.1 13.1 %collective-permute-start.43 = (f32[1,8,1,512]{3,2,1,0:T(1,128)S(1)}, f32[1,8,1,512]{3,2,1,0:T(1,128)S(1)}, u32[]{:S(2)}, u32[]{:S(2)}) collective-permute-start(f32[1,8,1,512]{3,2,1,0:T(1,128)S(1)} %get-tuple-element.46), channel_id=1, source_target_pairs={{4,0},{8,4},{12,8},{16,12},{20,16},{24,20},{28,24},{32,28},{36,32}... | collective-permute-start | bytes 49160 | tf_op jit(solution)/shard_map/ppermute | solution.py:25
  1144.2 6.6 collective-permute-start.42
  1145.6 10.7 collective-permute-start.40
  1147.5 5.2 collective-permute-start.38
  1150.8 5.5 collective-permute-start.39
  1156.6 6.1 collective-permute-start.47
  1156.7 13.4 %collective-permute-start.49 = (f32[1,8,1,512]{3,2,1,0:T(1,128)S(1)}, f32[1,8,1,512]{3,2,1,0:T(1,128)S(1)}, u32[]{:S(2)}, u32[]{:S(2)}) collective-permute-start(f32[1,8,1,512]{3,2,1,0:T(1,128)S(1)} %get-tuple-element.42), channel_id=1, source_target_pairs={{4,0},{8,4},{12,8},{16,12},{20,16},{24,20},{28,24},{32,28},{36,32}... | collective-permute-start | bytes 49160 | tf_op jit(solution)/shard_map/ppermute | solution.py:25
  1162.7 6.9 collective-permute-start.48
  1164.4 10.7 collective-permute-start.46
  1166.3 5.2 collective-permute-start.44
  1169.6 5.5 collective-permute-start.45
  1175.4 6.3 collective-permute-start.53
  1175.5 13.5 %collective-permute-start.55 = (f32[1,8,1,512]{3,2,1,0:T(1,128)S(1)}, f32[1,8,1,512]{3,2,1,0:T(1,128)S(1)}, u32[]{:S(2)}, u32[]{:S(2)}) collective-permute-start(f32[1,8,1,512]{3,2,1,0:T(1,128)S(1)} %get-tuple-element.38), channel_id=1, source_target_pairs={{4,0},{8,4},{12,8},{16,12},{20,16},{24,20},{28,24},{32,28},{36,32}... | collective-permute-start | bytes 49160 | tf_op jit(solution)/shard_map/ppermute | solution.py:25
  1181.7 6.9 collective-permute-start.54
  1183.2 10.9 collective-permute-start.52
  1185.1 5.4 collective-permute-start.50
  1188.6 5.5 collective-permute-start.51
  (4 other events, 6.1 us)
Sparse Core Ops, SparseCore 0:
  109.9 72.6 all-gather.2
  968.7 146.8 all-reduce.2
where the time goes:
time: 1200 us
  local copies, waits for them, and re-layouts  453 us (38%)
  other arithmetic  352 us (29%)
  waiting for transfers between devices  265 us (22%)
  starting transfers between devices  117 us (10%)
  between operations  15.1 us (1%)
    gather x1, local copies, waits for them, and re-layouts, local(): jnp.take_along_axis(lax.all_gather(other_surface, 'lat', axis=0, tiled=Tr...  258 us
    gather x1, local copies, waits for them, and re-layouts, local(): outgoing = live_weight * jnp.take(residual_surface, placed)  181 us
    scatter-add x1, other arithmetic, local(): jax.ops.segment_sum(outgoing.reshape(-1), segment_ids.reshape(-1), num_se...  172 us
    scatter-add x1, other arithmetic, local(): jax.ops.segment_sum((live_weight * values).reshape(-1), placed.reshape(-1...  171 us
    unnamed x3, waiting for transfers between devices  146 us
    ppermute x18, starting transfers between devices, extended(): lax.ppermute(head, axis, [((i + 1) % count, i) for i in range(ends)])  74 us
    all_gather x1, waiting for transfers between devices, local(): lax.all_gather(other_surface, 'lat', axis=0, tiled=True)  71.1 us
    ppermute x18, waiting for transfers between devices, extended(): lax.ppermute(tail, axis, [(i, (i + 1) % count) for i in range(ends)])  28.6 us
  transfers between devices with their start and end apart: 58, of which 22 were waited for; matrix products, arithmetic and copies ran while one was open for 1% of the time, Pallas kernels for 0%

commit v1 on v0

--- a/solution.py
+++ b/solution.py
@@ -96,7 +96,11 @@
     other_surface = partner_2(surface[None, :], "comp", 0)
     chosen = pulled
     values = jnp.take_along_axis(
-        lax.all_gather(other_surface, "lat", axis=0, tiled=True), chosen, axis=1
+        jnp.concatenate(
+            lax.all_to_all(jnp.stack([other_surface] * lax.axis_size("lat")), "lat", 0, 0), axis=0
+        ),
+        chosen,
+        axis=1,
     )
     income = jax.ops.segment_sum(
         (live_weight * values).reshape(-1), placed.reshape(-1), num_segments=cells

time: 1200 us -> 1170 us (0.975)
  waiting for transfers between devices: 265 us -> 213 us
    all_gather x1 -> x0, waiting for transfers between devices: 71.1 us -> none  [local(): lax.all_gather(other_surface, 'lat', axis=0, tiled=True)]
    all_to_all x0 -> x1, waiting for transfers between devices: none -> 21 us  [local(): lax.all_to_all(jnp.stack([other_surface] * lax.axis_size('lat')), 'lat',...]
    unnamed x3 -> x2, waiting for transfers between devices: 146 us -> 144 us
where the time goes in v1:
time: 1170 us; the launch traced here: 1160 us
  local copies, waits for them, and re-layouts  457 us (39%)
  other arithmetic  352 us (30%)
  waiting for transfers between devices  213 us (18%)
  starting transfers between devices  126 us (11%)
  between operations  15.4 us (1%)
    gather x1, local copies, waits for them, and re-layouts, local(): jnp.take_along_axis(jnp.concatenate(lax.all_to_all(jnp.stack([other_surfa...  258 us
    gather x1, local copies, waits for them, and re-layouts, local(): outgoing = live_weight * jnp.take(residual_surface, placed)  181 us
    scatter-add x1, other arithmetic, local(): jax.ops.segment_sum(outgoing.reshape(-1), segment_ids.reshape(-1), num_se...  172 us
    scatter-add x1, other arithmetic, local(): jax.ops.segment_sum((live_weight * values).reshape(-1), placed.reshape(-1...  171 us
    unnamed x2, waiting for transfers between devices  144 us
    ppermute x18, starting transfers between devices, extended(): lax.ppermute(head, axis, [((i + 1) % count, i) for i in range(ends)])  74 us
    ppermute x18, waiting for transfers between devices, extended(): lax.ppermute(tail, axis, [(i, (i + 1) % count) for i in range(ends)])  29.1 us
  transfers between devices with their start and end apart: 58, of which 22 were waited for; matrix products, arithmetic and copies ran while one was open for 1% of the time, Pallas kernels for 0%

profile of v1, /device:TPU:8, one launch (start us, length us, event | category | flops | bytes accessed | tf_op | source)
XLA Modules:
  0.0 1162.8 jit_solution(1563135053611998159)
XLA Ops:
  9.0 1.6 collective-permute-start.6
  10.6 3.8 collective-permute-start.4
  16.0 3.8 collective-permute-start.5
  19.9 4.1 collective-permute-start.11
  25.9 3.1 collective-permute-start.10
  29.2 2.1 collective-permute-done.10
  31.3 3.6 collective-permute-start.8
  35.4 2.8 collective-permute-start
  39.0 4.6 collective-permute-done.7
  44.0 3.3 collective-permute-start.1
  47.5 1.7 collective-permute-done.2
  49.2 3.7 collective-permute-done.3
  53.5 3.9 collective-permute-start.17
  57.4 1.4 collective-permute-start.16
  59.0 1.9 collective-permute-start.14
  60.9 3.4 collective-permute-start.12
  64.8 1.4 collective-permute-done.12
  66.2 3.6 collective-permute-done.13
  70.2 6.0 collective-permute-start.23
  76.2 1.5 collective-permute-start.22
  77.9 1.9 collective-permute-start.20
  79.8 3.3 collective-permute-start.18
  85.0 4.1 collective-permute-done.19
  89.6 5.9 collective-permute-start.29
  95.5 1.2 collective-permute-start.28
  96.8 1.9 collective-permute-start.26
  98.7 3.6 collective-permute-start.24
  102.8 1.4 collective-permute-done.24
  104.3 3.6 collective-permute-done.25
  108.3 1.2 collective-permute-done.30
  109.5 1.9 stack.2
  111.4 8.9 all-to-all-start
  125.8 21.0 %all-to-all-done = f32[32,1,8192]{2,1,0:T(1,128)S(1)} async-done(((f32[32,1,8192]{2,1,0:T(1,128)}), f32[32,1,8192]{2,1,0:T(1,128)S(1)}, u32[]{:S(2)}, u32[]{:S(2)}) %all-to-all-start) | async-done | bytes 1048608 | tf_op jit(solution)/shard_map/all_to_all | solution.py:100
  147.4 258.4 %gather_fusion.1 = f32[32768]{0:T(1024)S(1)} fusion(f32[32,8192]{1,0:T(8,128)S(1)} %bitcast.88, s32[32768]{0:T(1024)S(1)} %bitcast.89), kind=kCustom, calls=%fused_computation.1 | custom fusion | bytes 524288 | tf_op jit(solution)/shard_map/jit(take_along_axis)/gather | solution.py:98
  406.0 171.1 %scatter_custom_fusion = f32[8192]{0:T(1024)S(1)} fusion(s32[32768]{0:T(1024)S(1)} %bitcast.94, f32[32768]{0:T(1024)S(1)} %select_multiply_fusion.1, f32[]{:T(128)} %constant.98.clone.1), kind=kCustom, calls=%fused_computation.200 | custom fusion | flops 32768 | bytes 32772 | tf_op jit(solution)/shard_map/scatter-add | solution.py:105
  578.2 180.5 %gather_fusion = f32[32768]{0:T(1024)S(1)} fusion(f32[8192]{0:T(1024)S(1)} %mul.242, s32[32768]{0:T(1024)S(1)} %copy-done.10), kind=kCustom, calls=%fused_computation | custom fusion | bytes 393216 | tf_op jit(solution)/shard_map/jit(_take)/gather | solution.py:111
  758.9 171.6 %scatter_custom_fusion.1 = f32[262144]{0:T(1024)S(1)} fusion(s32[32768]{0:T(1024)} %bitcast.105, f32[32768]{0:T(1024)S(1)} %select_multiply_fusion, f32[]{:T(128)} %constant.98.clone.1), kind=kCustom, calls=%fused_computation.9 | custom fusion | flops 32768 | bytes 1049088 | tf_op jit(solution)/shard_map/scatter-add | solution.py:114
  932.9 143.5 %all-reduce.3.cloned.1.call-done = f32[32,8192]{1,0:T(8,128)} async-done(((f32[32,8192]{1,0:T(8,128)}), f32[32,8192]{1,0:T(8,128)}) %all-reduce.3.cloned.1.call-update) | async-done | bytes 1048592
  1076.4 1.6 constant_dynamic-slice_fusion
  1080.6 1.6 collective-permute-start.35
  1082.2 4.9 collective-permute-start.37
  1087.2 2.9 collective-permute-start.36
  1090.2 1.9 collective-permute-start.34
  1092.8 1.5 collective-permute-start.33
  1094.7 1.8 collective-permute-done.32
  1096.5 1.8 collective-permute-done.33
  1098.9 6.0 collective-permute-start.43
  1104.9 1.3 collective-permute-start.42
  1106.3 1.9 collective-permute-start.40
  1108.3 3.3 collective-permute-start.38
  1112.0 1.4 collective-permute-done.38
  1113.5 3.6 collective-permute-done.39
  1117.5 6.0 collective-permute-start.49
  1123.5 1.5 collective-permute-start.48
  1125.1 1.9 collective-permute-start.46
  1127.1 3.3 collective-permute-start.44
  1130.9 1.4 collective-permute-done.44
  1132.3 3.6 collective-permute-done.45
  1136.3 6.2 collective-permute-start.55
  1142.5 1.4 collective-permute-start.54
  1143.9 1.9 collective-permute-start.52
  1145.9 3.5 collective-permute-start.50
  1149.8 1.4 collective-permute-done.50
  1151.3 3.6 collective-permute-done.51
  (186 shorter events, 29.7 us)
Async XLA Ops:
  9.0 29.2 %collective-permute-start.6 = (f32[1,9,1,512]{3,2,1,0:T(1,128)S(1)}, f32[1,9,1,512]{3,2,1,0:T(1,128)S(1)}, u32[]{:S(2)}, u32[]{:S(2)}) collective-permute-start(f32[1,9,1,512]{3,2,1,0:T(1,128)S(1)} %get-tuple-element.37), channel_id=1, source_target_pairs={{0,1},{1,0},{2,3},{3,2},{4,5},{5,4},{6,7},{7,6},{8,9},{9,8},{10,11... | collective-permute-start | bytes 55304 | tf_op jit(solution)/shard_map/ppermute | solution.py:12
  10.6 38.5 %collective-permute-start.4 = (f32[1,9,1,512]{3,2,1,0:T(1,128)S(1)}, f32[1,9,1,512]{3,2,1,0:T(1,128)S(1)}, u32[]{:S(2)}, u32[]{:S(2)}) collective-permute-start(f32[1,9,1,512]{3,2,1,0:T(1,128)S(1)} %get-tuple-element.37), channel_id=1, source_target_pairs={{0,4},{4,8},{8,12},{12,16},{16,20},{20,24},{24,28},{28,32},{32,36}... | collective-permute-start | bytes 55304 | tf_op jit(solution)/shard_map/ppermute | solution.py:23
  15.4 10.5 collective-permute-start.9
  16.0 36.9 %collective-permute-start.5 = (f32[1,8,1,512]{3,2,1,0:T(1,128)S(1)}, f32[1,8,1,512]{3,2,1,0:T(1,128)S(1)}, u32[]{:S(2)}, u32[]{:S(2)}) collective-permute-start(f32[1,8,1,512]{3,2,1,0:T(1,128)S(1)} %get-tuple-element.67), channel_id=1, source_target_pairs={{0,4},{4,8},{8,12},{12,16},{16,20},{20,24},{24,28},{28,32},{32,36}... | collective-permute-start | bytes 49160 | tf_op jit(solution)/shard_map/ppermute | solution.py:23
  19.9 15.5 %collective-permute-start.11 = (f32[1,8,1,512]{3,2,1,0:T(1,128)S(1)}, f32[1,8,1,512]{3,2,1,0:T(1,128)S(1)}, u32[]{:S(2)}, u32[]{:S(2)}) collective-permute-start(f32[1,8,1,512]{3,2,1,0:T(1,128)S(1)} %get-tuple-element.66), channel_id=1, source_target_pairs={{4,0},{8,4},{12,8},{16,12},{20,16},{24,20},{28,24},{32,28},{36,32}... | collective-permute-start | bytes 49160 | tf_op jit(solution)/shard_map/ppermute | solution.py:25
  25.9 5.3 collective-permute-start.10
  31.3 12.8 %collective-permute-start.8 = (f32[1,9,1,512]{3,2,1,0:T(1,128)S(1)}, f32[1,9,1,512]{3,2,1,0:T(1,128)S(1)}, u32[]{:S(2)}, u32[]{:S(2)}) collective-permute-start(f32[1,9,1,512]{3,2,1,0:T(1,128)S(1)} %get-tuple-element.36), channel_id=1, source_target_pairs={{4,0},{8,4},{12,8},{16,12},{20,16},{24,20},{28,24},{32,28},{36,32}... | collective-permute-start | bytes 55304 | tf_op jit(solution)/shard_map/ppermute | solution.py:25
  35.4 12.0 %collective-permute-start = (f32[1,9,16,1]{3,2,1,0:T(8,128)S(1)}, f32[1,9,16,1]{3,2,1,0:T(8,128)S(1)}, u32[]{:S(2)}, u32[]{:S(2)}) collective-permute-start(f32[1,9,16,1]{3,2,1,0:T(8,128)S(1)} %get-tuple-element.35), channel_id=1, source_target_pairs={{1,0},{2,1},{3,2},{0,3},{5,4},{6,5},{7,6},{4,7},{9,8},{10,9},{11,1... | collective-permute-start | bytes 1736 | tf_op jit(solution)/shard_map/ppermute | solution.py:25
  38.2 5.4 collective-permute-start.7
  43.6 5.6 collective-permute-start.2
  44.0 5.2 collective-permute-start.1
  47.4 5.6 collective-permute-start.3
  53.4 4.0 collective-permute-start.15
  53.5 11.3 collective-permute-start.17
  57.4 6.9 collective-permute-start.16
  59.0 10.8 collective-permute-start.14
  60.9 5.3 collective-permute-start.12
  64.3 5.5 collective-permute-start.13
  70.1 6.1 collective-permute-start.21
  70.2 13.8 %collective-permute-start.23 = (f32[1,8,1,512]{3,2,1,0:T(1,128)S(1)}, f32[1,8,1,512]{3,2,1,0:T(1,128)S(1)}, u32[]{:S(2)}, u32[]{:S(2)}) collective-permute-start(f32[1,8,1,512]{3,2,1,0:T(1,128)S(1)} %get-tuple-element.58), channel_id=1, source_target_pairs={{4,0},{8,4},{12,8},{16,12},{20,16},{24,20},{28,24},{32,28},{36,32}... | collective-permute-start | bytes 49160 | tf_op jit(solution)/shard_map/ppermute | solution.py:25
  76.2 7.3 collective-permute-start.22
  77.9 11.3 collective-permute-start.20
  79.8 5.2 collective-permute-start.18
  83.1 6.0 collective-permute-start.19
  89.4 6.0 collective-permute-start.27
  89.6 13.2 %collective-permute-start.29 = (f32[1,8,1,512]{3,2,1,0:T(1,128)S(1)}, f32[1,8,1,512]{3,2,1,0:T(1,128)S(1)}, u32[]{:S(2)}, u32[]{:S(2)}) collective-permute-start(f32[1,8,1,512]{3,2,1,0:T(1,128)S(1)} %get-tuple-element.54), channel_id=1, source_target_pairs={{4,0},{8,4},{12,8},{16,12},{20,16},{24,20},{28,24},{32,28},{36,32}... | collective-permute-start | bytes 49160 | tf_op jit(solution)/shard_map/ppermute | solution.py:25
  95.5 6.9 collective-permute-start.28
  96.8 11.1 collective-permute-start.26
  98.7 5.6 collective-permute-start.24
  102.3 5.5 collective-permute-start.25
  108.2 1.3 collective-permute-start.30
  111.4 35.3 %all-to-all-start = ((f32[32,1,8192]{2,1,0:T(1,128)}), f32[32,1,8192]{2,1,0:T(1,128)S(1)}, u32[]{:S(2)}, u32[]{:S(2)}) async-start(f32[32,1,8192]{2,1,0:T(1,128)} %stack.2), calls=%async_computation | async-start | bytes 2097152 | tf_op jit(solution)/shard_map/all_to_all | solution.py:100
  120.3 956.1 %all-reduce.3.cloned.1.call-start = ((), (), s32[]{:S(2)}) async-start(), calls=%async_computation.1 | async-start | bytes 2097152
  147.4 258.5 %copy-start.5 = (f32[4,8,8,128]{3,1,2,0:T(8,128)S(1)}, f32[4,8,8,128]{3,1,2,0:T(8,128)}, u32[]{:S(2)}) copy-start(f32[4,8,8,128]{3,1,2,0:T(8,128)} %copy.14) | copy-start | bytes 393220
  147.4 258.5 %copy-start.8 = (s32[4,8,8,128]{3,1,2,0:T(8,128)S(1)}, s32[4,8,8,128]{3,1,2,0:T(8,128)}, u32[]{:S(2)}) copy-start(s32[4,8,8,128]{3,1,2,0:T(8,128)} %copy.15) | copy-start | bytes 393220
  147.4 258.5 %copy-start.11 = (pred[4,8,8,128]{3,1,2,0:T(8,128)(4,1)S(1)}, pred[4,8,8,128]{3,1,2,0:T(8,128)(4,1)}, u32[]{:S(2)}) copy-start(pred[4,8,8,128]{3,1,2,0:T(8,128)(4,1)} %copy.13) | copy-start | bytes 98308
  147.4 258.6 %copy-start.7 = (s32[4,8,8,128]{3,1,2,0:T(8,128)S(1)}, s32[4,8,8,128]{3,1,2,0:T(8,128)}, u32[]{:S(2)}) copy-start(s32[4,8,8,128]{3,1,2,0:T(8,128)} %copy.12) | copy-start | bytes 393220
  147.4 429.6 %copy-start.13 = (f32[2,4,8,128]{3,1,2,0:T(4,128)S(1)}, f32[2,4,8,128]{3,1,2,0:T(4,128)}, u32[]{:S(2)}) copy-start(f32[2,4,8,128]{3,1,2,0:T(4,128)} %copy.11) | copy-start | bytes 98308
  147.4 429.7 %copy-start.3 = (f32[1,8,16,512]{3,2,1,0:T(8,128)S(1)}, f32[1,8,16,512]{3,2,1,0:T(8,128)}, u32[]{:S(2)}) copy-start(f32[1,8,16,512]{3,2,1,0:T(8,128)} %copy-done.2) | copy-start | bytes 786436
  1078.0 1.3 collective-permute-start.31
  1080.6 6.5 collective-permute-start.35
  1082.2 12.5 %collective-permute-start.37 = (f32[1,8,1,512]{3,2,1,0:T(1,128)S(1)}, f32[1,8,1,512]{3,2,1,0:T(1,128)S(1)}, u32[]{:S(2)}, u32[]{:S(2)}) collective-permute-start(f32[1,8,1,512]{3,2,1,0:T(1,128)S(1)} %get-tuple-element.50), channel_id=1, source_target_pairs={{4,0},{8,4},{12,8},{16,12},{20,16},{24,20},{28,24},{32,28},{36,32}... | collective-permute-start | bytes 49160 | tf_op jit(solution)/shard_map/ppermute | solution.py:25
  1087.2 7.1 collective-permute-start.36
  1090.2 8.0 collective-permute-start.34
  1092.1 4.3 collective-permute-start.32
  1092.8 5.5 collective-permute-start.33
  1098.5 6.4 collective-permute-start.41
  1098.9 13.1 %collective-permute-start.43 = (f32[1,8,1,512]{3,2,1,0:T(1,128)S(1)}, f32[1,8,1,512]{3,2,1,0:T(1,128)S(1)}, u32[]{:S(2)}, u32[]{:S(2)}) collective-permute-start(f32[1,8,1,512]{3,2,1,0:T(1,128)S(1)} %get-tuple-element.46), channel_id=1, source_target_pairs={{4,0},{8,4},{12,8},{16,12},{20,16},{24,20},{28,24},{32,28},{36,32}... | collective-permute-start | bytes 49160 | tf_op jit(solution)/shard_map/ppermute | solution.py:25
  1104.9 6.6 collective-permute-start.42
  1106.3 10.7 collective-permute-start.40
  1108.3 5.2 collective-permute-start.38
  1111.6 5.5 collective-permute-start.39
  1117.4 6.1 collective-permute-start.47
  1117.5 13.4 %collective-permute-start.49 = (f32[1,8,1,512]{3,2,1,0:T(1,128)S(1)}, f32[1,8,1,512]{3,2,1,0:T(1,128)S(1)}, u32[]{:S(2)}, u32[]{:S(2)}) collective-permute-start(f32[1,8,1,512]{3,2,1,0:T(1,128)S(1)} %get-tuple-element.42), channel_id=1, source_target_pairs={{4,0},{8,4},{12,8},{16,12},{20,16},{24,20},{28,24},{32,28},{36,32}... | collective-permute-start | bytes 49160 | tf_op jit(solution)/shard_map/ppermute | solution.py:25
  1123.5 6.9 collective-permute-start.48
  1125.1 10.7 collective-permute-start.46
  1127.1 5.2 collective-permute-start.44
  1130.4 5.5 collective-permute-start.45
  1136.2 6.3 collective-permute-start.53
  1136.3 13.5 %collective-permute-start.55 = (f32[1,8,1,512]{3,2,1,0:T(1,128)S(1)}, f32[1,8,1,512]{3,2,1,0:T(1,128)S(1)}, u32[]{:S(2)}, u32[]{:S(2)}) collective-permute-start(f32[1,8,1,512]{3,2,1,0:T(1,128)S(1)} %get-tuple-element.38), channel_id=1, source_target_pairs={{4,0},{8,4},{12,8},{16,12},{20,16},{24,20},{28,24},{32,28},{36,32}... | collective-permute-start | bytes 49160 | tf_op jit(solution)/shard_map/ppermute | solution.py:25
  1142.5 6.9 collective-permute-start.54
  1143.9 10.9 collective-permute-start.52
  1145.9 5.4 collective-permute-start.50
  1149.4 5.5 collective-permute-start.51
  (12 other events, 761.5 us)
Sparse Core Ops, SparseCore 0:
  931.8 144.5 all-reduce.2
